TPU v7x, 32 devices: a whole 2x2x4 slice. The times are simulated.
32 devices in a mesh: ctx: 4 (over x, core), fsdp: 8 (over z, y).
Axes of the slice: x: 2, y: 2, z: 4, core: 2. Of those that a mesh axis runs over, the one named last changes fastest.
Arguments:
- tokens_in: bfloat16 [8, 1024, 1600], P('fsdp', 'ctx'), may hold values from -6 to 6
- group_order: int32 [8], replicated, may hold values from 0 to 7, each once
- out_grad: bfloat16 [8, 1024, 1600], P('fsdp', 'ctx'), may hold values from -6 to 6
- w_qkv: bfloat16 [1600, 4800], P('fsdp'), may hold values from -0.15625 to 0.15625
- w_attn_out: bfloat16 [1600, 1600], P('fsdp'), may hold values from -0.625 to 0.625
- b_query: bfloat16 [1600], P('fsdp'), may hold values from -3 to 3
- b_value: bfloat16 [1600], P('fsdp'), may hold values from -3 to 3
- b_attn_out: bfloat16 [1600], P('fsdp'), may hold values from -3 to 3
- w_fc: bfloat16 [1600, 6400], P('fsdp'), may hold values from -0.15625 to 0.15625
- w_proj: bfloat16 [6400, 1600], P('fsdp'), may hold values from -0.078125 to 0.078125
- b_fc: bfloat16 [6400], P('fsdp'), may hold values from -3 to 3
- b_proj: bfloat16 [1600], P('fsdp'), may hold values from -3 to 3
- ln1_gain: bfloat16 [1600], P('fsdp'), may hold values from 0.5 to 1.5
- ln1_bias: bfloat16 [1600], P('fsdp'), may hold values from -2 to 2
- ln2_gain: bfloat16 [1600], P('fsdp'), may hold values from 0.5 to 1.5
- ln2_bias: bfloat16 [1600], P('fsdp'), may hold values from -2 to 2
Outputs:
- tokens_out: bfloat16 [8, 1024, 1600], P('fsdp', 'ctx')
- grad_tokens: float32 [8, 1024, 1600], P('fsdp', 'ctx')
- grad_w_qkv: float32 [1600, 4800], P('fsdp')
- grad_w_attn_out: float32 [1600, 1600], P('fsdp')
- grad_b_query: float32 [1600], P('fsdp')
- grad_b_value: float32 [1600], P('fsdp')
- grad_b_attn_out: float32 [1600], P('fsdp')
- grad_w_fc: float32 [1600, 6400], P('fsdp')
- grad_w_proj: float32 [6400, 1600], P('fsdp')
- grad_b_fc: float32 [6400], P('fsdp')
- grad_b_proj: float32 [1600], P('fsdp')
- grad_ln1_gain: float32 [1600], P('fsdp')
- grad_ln1_bias: float32 [1600], P('fsdp')
- grad_ln2_gain: float32 [1600], P('fsdp')
- grad_ln2_bias: float32 [1600], P('fsdp')
Inputs may be any that keep to these rules, and one draw needn't show every extreme that they name: group_order is a permutation: each of the 8 groups of a sequence is stored at exactly one slot.
All inputs are finite; a program needn't handle non-finite values.
Results may differ from a plain program's by a relative error of at most 0.02.
Values may be sent and summed in bfloat16 or wider, within the bound.
No kernel may reach another device: no remote copies, remote signals or barrier semaphores. Data moves between devices by JAX's collectives and lax.ppermute only.
A program may use at most 384 MiB of HBM per device.

v0:
```python
import jax
import jax.numpy as jnp
from jax import lax
from jax.sharding import PartitionSpec as P

H = 25
GROUP = 128
norm_eps = 1e-05
masked_low = -1e30


def shifted(block, axis, distance):
    devices = range(lax.axis_size(axis))
    route = [((i - distance) % len(devices), i) for i in devices]
    return lax.ppermute(block, axis, route)


def layer_norm(values, norm_gain, norm_shift):
    centre = values - jnp.mean(values, axis=-1, keepdims=True)
    spread = jnp.mean(centre * centre, axis=-1, keepdims=True)
    return centre * lax.rsqrt(spread + norm_eps) * norm_gain + norm_shift


def gelu_tanh(values):
    return (
        0.5
        * values
        * (1.0 + jnp.tanh(0.7978845608028654 * (values + 0.044715 * values * values * values)))
    )


def outer_sum(left_op, right_op):
    return lax.dot_general(
        left_op, right_op, (((0,), (0,)), ((), ())), preferred_element_type=jnp.float32
    )


def back_product(left_op, right_op):
    return lax.dot_general(
        left_op, right_op, (((1,), (1,)), ((), ())), preferred_element_type=jnp.float32
    )


def block_positions(group_order, owner_index):
    slot_groups = lax.dynamic_slice_in_dim(group_order, 2 * owner_index, 2)
    offsets = jnp.arange(GROUP, dtype=jnp.int32)
    return (slot_groups[:, None] * GROUP + offsets[None, :]).reshape(-1)


def block_scores(queries, key_block, query_places, key_places):
    scale_factor = queries.shape[2] ** (-0.5)
    scores = (
        jnp.einsum("qhd,khd->hqk", queries, key_block, preferred_element_type=jnp.float32)
        * scale_factor
    )
    allowed = query_places[:, None] >= key_places[None, :]
    return (scores, allowed)


def stat_update(softmax_stats, scores, allowed):
    row_peak, row_mass = softmax_stats
    masked = jnp.where(allowed[None], scores, masked_low)
    new_peak = jnp.maximum(row_peak, jnp.max(masked, axis=2))
    weights = jnp.where(allowed[None], jnp.exp(masked - new_peak[:, :, None]), 0.0)
    return (new_peak, row_mass * jnp.exp(row_peak - new_peak) + jnp.sum(weights, axis=2))


def block_probs(scores, allowed, log_mass):
    return jnp.exp(jnp.where(allowed[None], scores - log_mass[:, :, None], masked_low))


def block_output(queries, pair_block, query_places, key_places, log_mass):
    scores, allowed = block_scores(queries, pair_block[:, 0], query_places, key_places)
    probs_low = block_probs(scores, allowed, log_mass).astype(jnp.bfloat16)
    return jnp.einsum(
        "hqk,khd->qhd", probs_low, pair_block[:, 1], preferred_element_type=jnp.float32
    )


def block_grads(queries, pair_block, query_places, key_places, log_mass, grad_attended, row_delta):
    key_block = pair_block[:, 0]
    value_block = pair_block[:, 1]
    scale_factor = queries.shape[2] ** (-0.5)
    scores, allowed = block_scores(queries, key_block, query_places, key_places)
    probs_full = block_probs(scores, allowed, log_mass)
    probs_low = probs_full.astype(jnp.bfloat16)
    grad_probs = jnp.einsum(
        "qhd,khd->hqk", grad_attended, value_block, preferred_element_type=jnp.float32
    )
    grad_scores = (probs_full * (grad_probs - row_delta[:, :, None]) * scale_factor).astype(
        jnp.bfloat16
    )
    grad_queries = jnp.einsum(
        "hqk,khd->qhd", grad_scores, key_block, preferred_element_type=jnp.float32
    )
    grad_keys = jnp.einsum("hqk,qhd->khd", grad_scores, queries, preferred_element_type=jnp.float32)
    grad_values = jnp.einsum(
        "hqk,qhd->khd", probs_low, grad_attended, preferred_element_type=jnp.float32
    )
    return (grad_queries, jnp.stack([grad_keys, grad_values], axis=1))


def per_device(
    tokens_in,
    group_order,
    out_grad,
    w_qkv,
    w_attn_out,
    b_query,
    b_value,
    b_attn_out,
    w_fc,
    w_proj,
    b_fc,
    b_proj,
    ln1_gain,
    ln1_bias,
    ln2_gain,
    ln2_bias,
):
    cycle_size = lax.axis_size("ctx")
    cycle_index = lax.axis_index("ctx")
    tokens = tokens_in[0].astype(jnp.float32)
    row_count = tokens.shape[0]
    model_width = tokens.shape[1]
    head_count = H
    head_dim = model_width // head_count
    qkv_full, attn_out_full, query_bias, value_bias, attn_out_bias, gain_one, shift_one = (
        lax.all_gather(w_qkv, "fsdp", axis=0, tiled=True),
        lax.all_gather(w_attn_out, "fsdp", axis=0, tiled=True),
        lax.all_gather(b_query, "fsdp", axis=0, tiled=True),
        lax.all_gather(b_value, "fsdp", axis=0, tiled=True),
        lax.all_gather(b_attn_out, "fsdp", axis=0, tiled=True),
        lax.all_gather(ln1_gain, "fsdp", axis=0, tiled=True),
        lax.all_gather(ln1_bias, "fsdp", axis=0, tiled=True),
    )
    normed, norm_pull = jax.vjp(
        layer_norm, tokens, gain_one.astype(jnp.float32), shift_one.astype(jnp.float32)
    )
    normed_low = normed.astype(jnp.bfloat16)
    mixed_all = jnp.dot(normed_low, qkv_full, preferred_element_type=jnp.float32)
    queries = (
        (mixed_all[:, :model_width] + query_bias.astype(jnp.float32))
        .astype(jnp.bfloat16)
        .reshape(row_count, head_count, head_dim)
    )
    pair_bias = jnp.concatenate(
        [jnp.zeros((model_width,), jnp.float32), value_bias.astype(jnp.float32)]
    )
    pair_local = (
        (mixed_all[:, model_width:] + pair_bias)
        .astype(jnp.bfloat16)
        .reshape(row_count, 2, head_count, head_dim)
    )
    query_places = block_positions(group_order, cycle_index)
    empty_peak = jnp.full((head_count, row_count), masked_low, jnp.float32)
    empty_mass = jnp.zeros((head_count, row_count), jnp.float32)
    first_scores, first_allowed = block_scores(
        queries, pair_local[:, 0], query_places, query_places
    )
    softmax_stats = stat_update((empty_peak, empty_mass), first_scores, first_allowed)

    def key_turn(cycle_turn, cycle_state):
        key_block, stats_now = cycle_state
        key_block = shifted(key_block, "ctx", 1)
        owner_index = (cycle_index - cycle_turn) % cycle_size
        scores, allowed = block_scores(
            queries, key_block, query_places, block_positions(group_order, owner_index)
        )
        return (key_block, stat_update(stats_now, scores, allowed))

    moved_keys, softmax_stats = lax.fori_loop(
        1, cycle_size, key_turn, (pair_local[:, 0], softmax_stats)
    )
    log_mass = softmax_stats[0] + jnp.log(softmax_stats[1])
    attended = block_output(queries, pair_local, query_places, query_places, log_mass)

    def pair_turn(cycle_turn, cycle_state):
        pair_block, output_now = cycle_state
        pair_block = shifted(pair_block, "ctx", 1)
        owner_index = (cycle_index - cycle_turn) % cycle_size
        return (
            pair_block,
            output_now
            + block_output(
                queries,
                pair_block,
                query_places,
                block_positions(group_order, owner_index),
                log_mass,
            ),
        )

    moved_pairs, attended = lax.fori_loop(1, cycle_size, pair_turn, (pair_local, attended))
    attended_low = attended.reshape(row_count, model_width).astype(jnp.bfloat16)
    branch = jnp.dot(
        attended_low, attn_out_full, preferred_element_type=jnp.float32
    ) + attn_out_bias.astype(jnp.float32)
    middle = tokens + branch
    fc_full, proj_full, fc_bias, proj_bias, gain_two, shift_two = (
        lax.all_gather(w_fc, "fsdp", axis=0, tiled=True),
        lax.all_gather(w_proj, "fsdp", axis=0, tiled=True),
        lax.all_gather(b_fc, "fsdp", axis=0, tiled=True),
        lax.all_gather(b_proj, "fsdp", axis=0, tiled=True),
        lax.all_gather(ln2_gain, "fsdp", axis=0, tiled=True),
        lax.all_gather(ln2_bias, "fsdp", axis=0, tiled=True),
    )
    normed_two, norm_two_pull = jax.vjp(
        layer_norm, middle, gain_two.astype(jnp.float32), shift_two.astype(jnp.float32)
    )
    normed_two_low = normed_two.astype(jnp.bfloat16)
    before = jnp.dot(normed_two_low, fc_full, preferred_element_type=jnp.float32) + fc_bias.astype(
        jnp.float32
    )
    activated, gelu_pull = jax.vjp(gelu_tanh, before)
    activated_low = activated.astype(jnp.bfloat16)
    branch_two = jnp.dot(
        activated_low, proj_full, preferred_element_type=jnp.float32
    ) + proj_bias.astype(jnp.float32)
    tokens_out = (middle + branch_two).astype(jnp.bfloat16)[None]
    fc_back, proj_back = (
        lax.all_gather(w_fc, "fsdp", axis=0, tiled=True),
        lax.all_gather(w_proj, "fsdp", axis=0, tiled=True),
    )
    grad_low = out_grad[0]
    grad_out = grad_low.astype(jnp.float32)
    grad_proj = outer_sum(activated_low, grad_low)
    grad_proj_bias = jnp.sum(grad_out, axis=0)
    (grad_before,) = gelu_pull(back_product(grad_low, proj_back))
    before_low = grad_before.astype(jnp.bfloat16)
    grad_fc = outer_sum(normed_two_low, before_low)
    grad_fc_bias = jnp.sum(before_low.astype(jnp.float32), axis=0)
    grad_middle_norm, grad_gain_two, grad_shift_two = norm_two_pull(
        back_product(before_low, fc_back)
    )
    grad_middle = grad_out + grad_middle_norm
    shard_fc, shard_proj, shard_fc_bias, shard_proj_bias, shard_gain_two, shard_shift_two = (
        lax.psum_scatter(
            grad_fc.astype(jnp.bfloat16), "fsdp", scatter_dimension=0, tiled=True
        ).astype(jnp.float32),
        lax.psum_scatter(
            grad_proj.astype(jnp.bfloat16), "fsdp", scatter_dimension=0, tiled=True
        ).astype(jnp.float32),
        lax.psum_scatter(
            grad_fc_bias.astype(jnp.bfloat16), "fsdp", scatter_dimension=0, tiled=True
        ).astype(jnp.float32),
        lax.psum_scatter(
            grad_proj_bias.astype(jnp.bfloat16), "fsdp", scatter_dimension=0, tiled=True
        ).astype(jnp.float32),
        lax.psum_scatter(
            grad_gain_two.astype(jnp.bfloat16), "fsdp", scatter_dimension=0, tiled=True
        ).astype(jnp.float32),
        lax.psum_scatter(
            grad_shift_two.astype(jnp.bfloat16), "fsdp", scatter_dimension=0, tiled=True
        ).astype(jnp.float32),
    )
    qkv_back, attn_out_back = (
        lax.all_gather(w_qkv, "fsdp", axis=0, tiled=True),
        lax.all_gather(w_attn_out, "fsdp", axis=0, tiled=True),
    )
    middle_low = grad_middle.astype(jnp.bfloat16)
    grad_attn_out = outer_sum(attended_low, middle_low)
    grad_attn_out_bias = jnp.sum(middle_low.astype(jnp.float32), axis=0)
    grad_attended = (
        back_product(middle_low, attn_out_back)
        .astype(jnp.bfloat16)
        .reshape(row_count, head_count, head_dim)
    )
    row_delta = jnp.einsum("qhd,qhd->hq", grad_attended.astype(jnp.float32), attended)

    def send_grads(grad_block):
        return shifted(grad_block.astype(jnp.bfloat16), "ctx", 1).astype(grad_block.dtype)

    grad_query_acc, grad_pair = block_grads(
        queries, pair_local, query_places, query_places, log_mass, grad_attended, row_delta
    )

    def back_turn(cycle_turn, cycle_state):
        pair_block, grad_block, query_now = cycle_state
        grad_block = send_grads(grad_block)
        pair_block = shifted(pair_block, "ctx", 1)
        owner_index = (cycle_index - cycle_turn) % cycle_size
        more_query, more_pair = block_grads(
            queries,
            pair_block,
            query_places,
            block_positions(group_order, owner_index),
            log_mass,
            grad_attended,
            row_delta,
        )
        return (pair_block, grad_block + more_pair, query_now + more_query)

    last_pair, grad_pair, grad_query_acc = lax.fori_loop(
        1, cycle_size, back_turn, (pair_local, grad_pair, grad_query_acc)
    )
    grad_pair = send_grads(grad_pair)
    grad_mixed_low = jnp.concatenate(
        [
            grad_query_acc.astype(jnp.bfloat16).reshape(row_count, model_width),
            grad_pair.astype(jnp.bfloat16).reshape(row_count, 2 * model_width),
        ],
        axis=1,
    )
    grad_qkv = outer_sum(normed_low, grad_mixed_low)
    grad_query_bias = jnp.sum(grad_mixed_low[:, :model_width].astype(jnp.float32), axis=0)
    grad_value_bias = jnp.sum(grad_mixed_low[:, 2 * model_width :].astype(jnp.float32), axis=0)
    grad_tokens_norm, grad_gain_one, grad_shift_one = norm_pull(
        back_product(grad_mixed_low, qkv_back)
    )
    grad_tokens = (grad_middle + grad_tokens_norm)[None]
    (
        shard_qkv,
        shard_attn_out,
        shard_query_bias,
        shard_value_bias,
        shard_attn_out_bias,
        shard_gain_one,
        shard_shift_one,
    ) = (
        lax.psum_scatter(
            grad_qkv.astype(jnp.bfloat16), "fsdp", scatter_dimension=0, tiled=True
        ).astype(jnp.float32),
        lax.psum_scatter(
            grad_attn_out.astype(jnp.bfloat16), "fsdp", scatter_dimension=0, tiled=True
        ).astype(jnp.float32),
        lax.psum_scatter(
            grad_query_bias.astype(jnp.bfloat16), "fsdp", scatter_dimension=0, tiled=True
        ).astype(jnp.float32),
        lax.psum_scatter(
            grad_value_bias.astype(jnp.bfloat16), "fsdp", scatter_dimension=0, tiled=True
        ).astype(jnp.float32),
        lax.psum_scatter(
            grad_attn_out_bias.astype(jnp.bfloat16), "fsdp", scatter_dimension=0, tiled=True
        ).astype(jnp.float32),
        lax.psum_scatter(
            grad_gain_one.astype(jnp.bfloat16), "fsdp", scatter_dimension=0, tiled=True
        ).astype(jnp.float32),
        lax.psum_scatter(
            grad_shift_one.astype(jnp.bfloat16), "fsdp", scatter_dimension=0, tiled=True
        ).astype(jnp.float32),
    )
    summed = (
        lax.psum(shard_qkv.astype(jnp.bfloat16), "ctx").astype(jnp.float32),
        lax.psum(shard_attn_out.astype(jnp.bfloat16), "ctx").astype(jnp.float32),
        lax.psum(shard_query_bias.astype(jnp.bfloat16), "ctx").astype(jnp.float32),
        lax.psum(shard_value_bias.astype(jnp.bfloat16), "ctx").astype(jnp.float32),
        lax.psum(shard_attn_out_bias.astype(jnp.bfloat16), "ctx").astype(jnp.float32),
        lax.psum(shard_fc.astype(jnp.bfloat16), "ctx").astype(jnp.float32),
        lax.psum(shard_proj.astype(jnp.bfloat16), "ctx").astype(jnp.float32),
        lax.psum(shard_fc_bias.astype(jnp.bfloat16), "ctx").astype(jnp.float32),
        lax.psum(shard_proj_bias.astype(jnp.bfloat16), "ctx").astype(jnp.float32),
        lax.psum(shard_gain_one.astype(jnp.bfloat16), "ctx").astype(jnp.float32),
        lax.psum(shard_shift_one.astype(jnp.bfloat16), "ctx").astype(jnp.float32),
        lax.psum(shard_gain_two.astype(jnp.bfloat16), "ctx").astype(jnp.float32),
        lax.psum(shard_shift_two.astype(jnp.bfloat16), "ctx").astype(jnp.float32),
    )
    return (
        tokens_out,
        grad_tokens,
        summed[0],
        summed[1],
        summed[2],
        summed[3],
        summed[4],
        summed[5],
        summed[6],
        summed[7],
        summed[8],
        summed[9],
        summed[10],
        summed[11],
        summed[12],
    )


def solution(mesh):
    placed = (
        P("fsdp", "ctx", None),
        P(),
        P("fsdp", "ctx", None),
        P("fsdp", None),
        P("fsdp", None),
        P("fsdp"),
        P("fsdp"),
        P("fsdp"),
        P("fsdp", None),
        P("fsdp", None),
        P("fsdp"),
        P("fsdp"),
        P("fsdp"),
        P("fsdp"),
        P("fsdp"),
        P("fsdp"),
    )
    return jax.shard_map(
        per_device,
        mesh=mesh,
        in_specs=placed,
        out_specs=(
            P("fsdp", "ctx", None),
            P("fsdp", "ctx", None),
            P("fsdp", None),
            P("fsdp", None),
            P("fsdp"),
            P("fsdp"),
            P("fsdp"),
            P("fsdp", None),
            P("fsdp", None),
            P("fsdp"),
            P("fsdp"),
            P("fsdp"),
            P("fsdp"),
            P("fsdp"),
            P("fsdp"),
        ),
        check_vma=False,
    )
```

profile of v0, /device:TPU:0, one launch (start us, length us, event | category | flops | bytes accessed | tf_op | source)
XLA Modules:
  0.0 2477.9 jit_solution(9812996042900565081)
XLA Ops:
  14.1 40.9 %all-reduce.22 = (bf16[1600]{0:T(1024)(128)(2,1)S(1)}, bf16[1600]{0:T(1024)(128)(2,1)S(1)}, bf16[1600]{0:T(1024)(128)(2,1)S(1)}, bf16[1600]{0:T(1024)(128)(2,1)S...) all-reduce(bf16[1600]{0:T(1024)(128)(2,1)S(1)} %dynamic-update-slic, ...), channel_id=1, replica_groups=mesh['ctx'=4,'fsdp'=8] {'fsdp'}, use_global_device_ids=true, to_apply=%add.2 | all-reduce | flops 17600 | bytes 70400
  56.0 170.8 %all-gather.5.cloned.1.call-done = bf16[1600,4800]{1,0:T(8,128)(2,1)} async-done(((bf16[200,4800]{1,0:T(8,128)(2,1)}), bf16[1600,4800]{1,0:T(8,128)(2,1)}) %all-gather.5.cloned.1.call-update) | async-done | bytes 15360016 | tf_op jit(solution)/shard_map/all_gather | solution.py:129
  226.7 14.8 fusion.79
  256.3 47.1 %while.58 = (s32[]{:T(128)}, bf16[256,25,64]{0,2,1:T(8,128)(2,1)}, f32[25,256]{1,0:T(8,128)S(1)}, f32[25,256]{1,0:T(8,128)S(1)}, s32[]{:T(128)}, /*index=5*/s32[...) while((s32[]{:T(128)}, bf16[256,25,64]{0,2,1:T(8,128)(2,1)}, ...), condition=%wide.region_7.8_spmd.clone, body=%wide.region_4.7_spmd.clone.sunk | while | flops 222901264 | bytes 20194680 | solution.py:172
  256.5 11.7 collective-permute-done
  272.2 11.7 collective-permute-done
  287.9 11.7 collective-permute-done
  309.2 84.4 %while.59 = (s32[]{:T(128)}, bf16[256,2,25,64]{0,3,2,1:T(8,128)(2,1)}, f32[256,25,64]{0,2,1:T(8,128)}, s32[]{:T(128)}, s32[8]{0:T(128)S(1)}, /*index=5*/bf16[256...) while((s32[]{:T(128)}, ...), condition=%wide.region_9.10_spmd.clone, body=%wide.region_8.9_spmd.clone.sunk | while | flops 426459680 | bytes 15725944 | solution.py:194
  309.5 20.5 collective-permute-done.1
  337.5 20.5 collective-permute-done.1
  365.6 20.5 collective-permute-done.1
  401.5 305.3 %all-gather.9.cloned.1.call-done = bf16[1600,6400]{1,0:T(8,128)(2,1)} async-done(((bf16[200,6400]{1,0:T(8,128)(2,1)}), bf16[1600,6400]{1,0:T(8,128)(2,1)}) %all-gather.9.cloned.1.call-update) | async-done | bytes 20480016 | tf_op jit(solution)/shard_map/all_gather | solution.py:201
  706.8 12.4 convolution_add_fusion
  719.2 396.9 %all-gather.11.cloned.1.call-done = bf16[6400,1600]{1,0:T(8,128)(2,1)} async-done(((bf16[800,1600]{1,0:T(8,128)(2,1)}), bf16[6400,1600]{1,0:T(8,128)(2,1)}) %all-gather.11.cloned.1.call-update) | async-done | bytes 20480016 | tf_op jit(solution)/shard_map/all_gather | solution.py:202
  1116.1 15.6 fusion.88
  1131.7 13.8 multiply_reduce_fusion
  1165.2 125.4 %while.60 = (s32[]{:T(128)}, bf16[256,2,25,64]{0,3,2,1:T(8,128)(2,1)}, bf16[256,2,25,64]{0,3,2,1:T(8,128)(2,1)}, f32[256,25,64]{0,2,1:T(8,128)}, s32[]{:T(128)},...) while((s32[]{:T(128)}, ...), condition=%wide.region_15.16_spmd.clone, body=%wide.region_14.15_spmd.clone.sunk | while | flops 1070350848 | bytes 81393160 | solution.py:294
  1167.5 18.8 collective-permute-done.2
  1209.2 18.8 collective-permute-done.2
  1250.8 18.8 collective-permute-done.2
  1279.7 7.6 collective-permute-done.3
  1292.3 19.0 collective-permute-done.4
  1311.3 8.3 convolution_convert_fusion.2
  1321.1 12.8 convolution_convert_fusion.1
  1335.0 13.7 convolution_convert_fusion
  1350.8 9.9 fusion.81
  1362.7 209.1 %reduce-scatter.9.cloned.1.call-done = bf16[200,4800]{1,0:T(8,128)(2,1)} async-done(((bf16[1600,4800]{1,0:T(8,128)(2,1)}), bf16[200,4800]{1,0:T(8,128)(2,1)}) %reduce-scatter.9.cloned.1.call-update) | async-done | bytes 1920016 | tf_op jit(solution)/shard_map/reduce_scatter | solution.py:321
  1571.8 389.9 %reduce-scatter.15.cloned.1.call-done = bf16[200,6400]{1,0:T(8,128)(2,1)} async-done(((bf16[1600,6400]{1,0:T(8,128)(2,1)}), bf16[200,6400]{1,0:T(8,128)(2,1)}) %reduce-scatter.15.cloned.1.call-update) | async-done | bytes 2560016
  1961.7 351.2 %reduce-scatter.11.cloned.1.call-done = bf16[800,1600]{1,0:T(8,128)(2,1)} async-done(((bf16[6400,1600]{1,0:T(8,128)(2,1)}), bf16[800,1600]{1,0:T(8,128)(2,1)}) %reduce-scatter.11.cloned.1.call-update) | async-done | bytes 2560016 | tf_op jit(solution)/shard_map/reduce_scatter | solution.py:241
  2314.5 35.7 %all-reduce.21 = (bf16[1600]{0:T(1024)(128)(2,1)S(1)}, bf16[1600]{0:T(1024)(128)(2,1)S(1)}, bf16[1600]{0:T(1024)(128)(2,1)S(1)}, bf16[1600]{0:T(1024)(128)(2,1)S...) all-reduce(bf16[1600]{0:T(1024)(128)(2,1)S(1)} %dynamic-update-slic, ...), channel_id=1, replica_groups=mesh['ctx'=4,'fsdp'=8] {'fsdp'}, use_global_device_ids=true, to_apply=%add.9 | all-reduce | flops 20800 | bytes 83200
  2366.8 17.4 fusion.44
  2384.3 76.2 %all-reduce.27.cloned.1.call-done = (bf16[200,4800]{1,0:T(8,128)(2,1)}, bf16[200,1600]{1,0:T(8,128)(2,1)}, bf16[200,6400]{1,0:T(8,128)(2,1)}, bf16[800,1600]{1,0:T(8,128)(2,1)}) async-done(((bf16[200,4800]{1,0:T(8,128)(2,1)}, bf16[200,1600]{1,0:T(8,128)(2,1)}, bf16[200,6400]{1,0:T(8,128)(2,1)}, bf16[800,1600]{1,0:T(8,128)(2,1)}), (bf16[200,4800]{1,0:T(8,128)(2,1)}, bf16[200,1600]{1,0:T(8,128)(2,1)}, ...) | async-done | bytes 7680016 | tf_op jit(solution)/shard_map/psum | solution.py:344
  (317 shorter events, 185.2 us)
Async XLA Ops:
  7.2 219.6 %all-gather.5.cloned.1.call-start = ((), (), s32[]{:S(2)}) async-start(), calls=%async_computation.4 | async-start | bytes 17510400 | tf_op jit(solution)/shard_map/all_gather | solution.py:129
  8.0 388.0 %all-gather.7.cloned.1.call-start = ((), (), s32[]{:S(2)}) async-start(), calls=%async_computation.5 | async-start | bytes 5990400 | tf_op jit(solution)/shard_map/all_gather | solution.py:130
  8.8 698.0 %all-gather.9.cloned.1.call-start = ((), (), s32[]{:S(2)}) async-start(), calls=%async_computation.6 | async-start | bytes 23040000 | tf_op jit(solution)/shard_map/all_gather | solution.py:201
  9.5 1106.6 %all-gather.11.cloned.1.call-start = ((), (), s32[]{:S(2)}) async-start(), calls=%async_computation.7 | async-start | bytes 23961600 | tf_op jit(solution)/shard_map/all_gather | solution.py:202
  10.1 1352.6 %reduce-scatter.13.cloned.1.call-start = ((), (), s32[]{:S(2)}) async-start(), calls=%async_computation.10 | async-start | bytes 5990400
  55.0 186.5 %copy-start.23 = (f32[1600]{0:T(1024)}, f32[1600]{0:T(1024)S(1)}, u32[]{:S(2)}) copy-start(f32[1600]{0:T(1024)S(1)} %convert_element_type.234) | copy-start | bytes 19204
  55.0 186.5 %copy-start.21 = (f32[1600]{0:T(1024)}, f32[1600]{0:T(1024)S(1)}, u32[]{:S(2)}) copy-start(f32[1600]{0:T(1024)S(1)} %convert_element_type.233) | copy-start | bytes 19204
  55.5 186.0 %copy-start.25 = (f32[256]{0:T(256)}, f32[256]{0:T(256)S(1)}, u32[]{:S(2)}) copy-start(f32[256]{0:T(256)S(1)} %broadcast_multiply_fusion.1) | copy-start | bytes 3076
  55.8 185.8 %copy-start.33 = (f32[256]{0:T(256)}, f32[256]{0:T(256)S(1)}, u32[]{:S(2)}) copy-start(f32[256]{0:T(256)S(1)} %fusion.55) | copy-start | bytes 3076
  55.8 185.7 %copy-start.27 = (f32[256]{0:T(256)}, f32[256]{0:T(256)S(1)}, u32[]{:S(2)}) copy-start(f32[256]{0:T(256)S(1)} %fusion.69) | copy-start | bytes 3076
  256.3 12.0 collective-permute-start
  272.0 12.0 collective-permute-start
  287.7 12.0 collective-permute-start
  309.2 20.8 collective-permute-start.1
  337.3 20.8 collective-permute-start.1
  365.4 20.8 collective-permute-start.1
  401.2 744.3 %copy-start.2 = (f32[256,1600]{0,1:T(8,128)}, f32[256,1600]{0,1:T(8,128)S(1)}, u32[]{:S(2)}) copy-start(f32[256,1600]{0,1:T(8,128)S(1)} %get-tuple-element.873) | copy-start | bytes 4915204
  1163.8 408.0 %reduce-scatter.9.cloned.1.call-start = ((), (), s32[]{:S(2)}) async-start(), calls=%async_computation.8 | async-start | bytes 17510400 | tf_op jit(solution)/shard_map/reduce_scatter | solution.py:321
  1165.1 146.2 %copy-start.22 = (f32[1600]{0:T(1024)S(1)}, f32[1600]{0:T(1024)}, u32[]{:S(2)}) copy-start(f32[1600]{0:T(1024)} %copy-done.21) | copy-start | bytes 19204
  1165.1 146.2 %copy-start.24 = (f32[1600]{0:T(1024)S(1)}, f32[1600]{0:T(1024)}, u32[]{:S(2)}) copy-start(f32[1600]{0:T(1024)} %copy-done.23) | copy-start | bytes 19204
  1165.1 146.2 %copy-start.26 = (f32[256]{0:T(256)S(1)}, f32[256]{0:T(256)}, u32[]{:S(2)}) copy-start(f32[256]{0:T(256)} %copy-done.25) | copy-start | bytes 3076
  1165.2 146.2 %copy-start.28 = (f32[256]{0:T(256)S(1)}, f32[256]{0:T(256)}, u32[]{:S(2)}) copy-start(f32[256]{0:T(256)} %copy-done.27) | copy-start | bytes 3076
  1165.6 20.8 collective-permute-start.2
  1165.6 38.4 %collective-permute-start.3 = (bf16[256,2,25,64]{0,3,2,1:T(8,128)(2,1)}, bf16[256,2,25,64]{0,3,2,1:T(8,128)(2,1)}, u32[]{:S(2)}, u32[]{:S(2)}) collective-permute-start(bf16[256,2,25,64]{0,3,2,1:T(8,128)(2,1)} %get-tuple-element.1158), channel_id=1, source_target_pairs={{24,0},{0,8},{8,16},{16,24},{25,1},{1,9},{9,17},{17,25},{26,2},{2,... | collective-permute-start | bytes 4915208 | tf_op jit(solution)/shard_map/while/body/eval_jaxpr/ppermute | solution.py:15
  1207.3 20.8 collective-permute-start.2
  1207.3 38.4 %collective-permute-start.3 = (bf16[256,2,25,64]{0,3,2,1:T(8,128)(2,1)}, bf16[256,2,25,64]{0,3,2,1:T(8,128)(2,1)}, u32[]{:S(2)}, u32[]{:S(2)}) collective-permute-start(bf16[256,2,25,64]{0,3,2,1:T(8,128)(2,1)} %get-tuple-element.1158), channel_id=1, source_target_pairs={{24,0},{0,8},{8,16},{16,24},{25,1},{1,9},{9,17},{17,25},{26,2},{2,... | collective-permute-start | bytes 4915208 | tf_op jit(solution)/shard_map/while/body/eval_jaxpr/ppermute | solution.py:15
  1248.9 20.8 collective-permute-start.2
  1248.9 38.4 %collective-permute-start.3 = (bf16[256,2,25,64]{0,3,2,1:T(8,128)(2,1)}, bf16[256,2,25,64]{0,3,2,1:T(8,128)(2,1)}, u32[]{:S(2)}, u32[]{:S(2)}) collective-permute-start(bf16[256,2,25,64]{0,3,2,1:T(8,128)(2,1)} %get-tuple-element.1158), channel_id=1, source_target_pairs={{24,0},{0,8},{8,16},{16,24},{25,1},{1,9},{9,17},{17,25},{26,2},{2,... | collective-permute-start | bytes 4915208 | tf_op jit(solution)/shard_map/while/body/eval_jaxpr/ppermute | solution.py:15
  1290.6 20.8 collective-permute-start.4
  1319.7 642.0 %reduce-scatter.15.cloned.1.call-start = ((), (), s32[]{:S(2)}) async-start(), calls=%async_computation.11 | async-start | bytes 23040000
  1333.9 979.0 %reduce-scatter.11.cloned.1.call-start = ((), (), s32[]{:S(2)}) async-start(), calls=%async_computation.9 | async-start | bytes 23961600 | tf_op jit(solution)/shard_map/reduce_scatter | solution.py:241
  1348.7 1111.8 %all-reduce.27.cloned.1.call-start = ((), (), s32[]{:S(2)}) async-start(), calls=%async_computation.12 | async-start | bytes 15667200 | tf_op jit(solution)/shard_map/psum | solution.py:344
  (46 other events, 313.9 us)
Sparse Core Ops, SparseCore 0:
  10.2 216.5 all-gather.4
  228.9 85.4 all-gather.6
  316.0 390.7 all-gather.8
  708.1 407.8 all-gather.10
  1163.9 124.0 reduce-scatter.12
  1319.8 251.9 reduce-scatter.8
  1575.3 386.3 reduce-scatter.14
  1965.4 347.5 reduce-scatter.10
  2315.6 144.8 all-reduce.26
where the time goes:
time: 2480 us
  waiting for transfers between devices  2100 us (85%)
  matrix products  193 us (8%)
  blocking collectives  83.6 us (3%)
  other arithmetic  52.9 us (2%)
  local copies, waits for them, and re-layouts  28.6 us (1%)
    all_gather x1, waiting for transfers between devices, per_device(): lax.all_gather(w_proj, 'fsdp', axis=0, tiled=True)  397 us
    unnamed x11, waiting for transfers between devices  393 us
    reduce_scatter x1, waiting for transfers between devices, per_device(): lax.psum_scatter(grad_proj.astype(jnp.bfloat16), 'fsdp', scatter_dimensio...  351 us
    all_gather x1, waiting for transfers between devices, per_device(): lax.all_gather(w_fc, 'fsdp', axis=0, tiled=True)  305 us
    reduce_scatter x1, waiting for transfers between devices, per_device(): lax.psum_scatter(grad_qkv.astype(jnp.bfloat16), 'fsdp', scatter_dimension...  209 us
    ppermute x13, waiting for transfers between devices, shifted(): return lax.ppermute(block, axis, route)  195 us
    all_gather x1, waiting for transfers between devices, per_device(): lax.all_gather(w_qkv, 'fsdp', axis=0, tiled=True)  171 us
    unnamed x2, blocking collectives  76.6 us
  transfers between devices with their start and end apart: 22, of which 20 were waited for; matrix products, arithmetic and copies ran while one was open for 8% of the time, Pallas kernels for 0%

commit v1 on v0

--- a/solution.py
+++ b/solution.py
@@ -7,6 +7,24 @@
 GROUP = 128
 norm_eps = 1e-05
 masked_low = -1e30
+
+
+def gather_around(shard, axis, dim):
+    ways, here, lap = (lax.axis_size(axis), lax.axis_index(axis), shard.shape[dim])
+    shape = [n * ways if d == dim else n for d, n in enumerate(shard.shape)]
+    full = lax.dynamic_update_slice_in_dim(
+        jnp.zeros(shape, shard.dtype), shard, here * lap, axis=dim
+    )
+    going_up = going_down = shard
+    for far in range(1, ways // 2 + 1):
+        going_up = lax.ppermute(going_up, axis, [(d, (d + 1) % ways) for d in range(ways)])
+        full = lax.dynamic_update_slice_in_dim(full, going_up, (here - far) % ways * lap, axis=dim)
+        if 2 * far < ways:
+            going_down = lax.ppermute(going_down, axis, [(d, (d - 1) % ways) for d in range(ways)])
+            full = lax.dynamic_update_slice_in_dim(
+                full, going_down, (here + far) % ways * lap, axis=dim
+            )
+    return full
 
 
 def shifted(block, axis, distance):
@@ -199,7 +217,7 @@
     middle = tokens + branch
     fc_full, proj_full, fc_bias, proj_bias, gain_two, shift_two = (
         lax.all_gather(w_fc, "fsdp", axis=0, tiled=True),
-        lax.all_gather(w_proj, "fsdp", axis=0, tiled=True),
+        gather_around(w_proj, "fsdp", 0),
         lax.all_gather(b_fc, "fsdp", axis=0, tiled=True),
         lax.all_gather(b_proj, "fsdp", axis=0, tiled=True),
         lax.all_gather(ln2_gain, "fsdp", axis=0, tiled=True),

time: 2480 us -> 2780 us (1.12)
  waiting for transfers between devices: 2100 us -> 2340 us
  local copies, waits for them, and re-layouts: 28.6 us -> 60.9 us
    ppermute x0 -> x7, waiting for transfers between devices: none -> 462 us  [the longest x4 459 us: gather_around(): lax.ppermute(going_up, axis, [(d, (d + 1) % ways) for d in range(ways)])]
    reduce_scatter x1, waiting for transfers between devices: 209 us -> 0.02 us  [per_device(): lax.psum_scatter(grad_qkv.astype(jnp.bfloat16), 'fsdp', scatter_dimension...]
  transfers between devices with their start and end apart: 22 -> 29, of which waited for: 20 -> 25; matrix products, arithmetic and copies ran while one was open for 8% -> 9% of each run, Pallas kernels for 0% -> 0%
where the time goes in v1:
time: 2780 us
  waiting for transfers between devices  2340 us (84%)
  matrix products  192 us (7%)
  blocking collectives  83.6 us (3%)
  local copies, waits for them, and re-layouts  60.9 us (2%)
  other arithmetic  53.1 us (2%)
    ppermute x4, waiting for transfers between devices, gather_around(): lax.ppermute(going_up, axis, [(d, (d + 1) % ways) for d in range(ways)])  459 us
    all_gather x1, waiting for transfers between devices, per_device(): lax.all_gather(w_proj, 'fsdp', axis=0, tiled=True)  397 us
    unnamed x11, waiting for transfers between devices  383 us
    reduce_scatter x1, waiting for transfers between devices, per_device(): lax.psum_scatter(grad_proj.astype(jnp.bfloat16), 'fsdp', scatter_dimensio...  351 us
    all_gather x1, waiting for transfers between devices, per_device(): lax.all_gather(w_fc, 'fsdp', axis=0, tiled=True)  306 us
    ppermute x13, waiting for transfers between devices, shifted(): return lax.ppermute(block, axis, route)  195 us
    all_gather x1, waiting for transfers between devices, per_device(): lax.all_gather(w_qkv, 'fsdp', axis=0, tiled=True)  171 us
    unnamed x2, blocking collectives  76.6 us
  transfers between devices with their start and end apart: 29, of which 25 were waited for; matrix products, arithmetic and copies ran while one was open for 9% of the time, Pallas kernels for 0%

profile of v1, /device:TPU:0, one launch (start us, length us, event | category | flops | bytes accessed | tf_op | source)
XLA Modules:
  0.0 2776.0 jit_solution(8959482860842083038)
XLA Ops:
  14.1 40.9 %all-reduce.22 = (bf16[1600]{0:T(1024)(128)(2,1)S(1)}, bf16[1600]{0:T(1024)(128)(2,1)S(1)}, bf16[1600]{0:T(1024)(128)(2,1)S(1)}, bf16[1600]{0:T(1024)(128)(2,1)S...) all-reduce(bf16[1600]{0:T(1024)(128)(2,1)S(1)} %dynamic-update-slic, ...), channel_id=1, replica_groups=mesh['ctx'=4,'fsdp'=8] {'fsdp'}, use_global_device_ids=true, to_apply=%add.2 | all-reduce | flops 17600 | bytes 70400
  56.0 170.8 %all-gather.5.cloned.1.call-done = bf16[1600,4800]{1,0:T(8,128)(2,1)} async-done(((bf16[200,4800]{1,0:T(8,128)(2,1)}), bf16[1600,4800]{1,0:T(8,128)(2,1)}) %all-gather.5.cloned.1.call-update) | async-done | bytes 15360016 | tf_op jit(solution)/shard_map/all_gather | solution.py:147
  226.7 14.8 fusion.79
  256.3 47.1 %while.58 = (s32[]{:T(128)}, bf16[256,25,64]{0,2,1:T(8,128)(2,1)}, f32[25,256]{1,0:T(8,128)S(1)}, f32[25,256]{1,0:T(8,128)S(1)}, s32[]{:T(128)}, /*index=5*/s32[...) while((s32[]{:T(128)}, bf16[256,25,64]{0,2,1:T(8,128)(2,1)}, ...), condition=%wide.region_7.8_spmd.clone, body=%wide.region_4.7_spmd.clone.sunk | while | flops 222901264 | bytes 20194680 | solution.py:190
  256.5 11.7 collective-permute-done
  272.2 11.7 collective-permute-done
  287.9 11.7 collective-permute-done
  309.0 84.4 %while.59 = (s32[]{:T(128)}, bf16[256,2,25,64]{0,3,2,1:T(8,128)(2,1)}, f32[256,25,64]{0,2,1:T(8,128)}, s32[]{:T(128)}, s32[8]{0:T(128)S(1)}, /*index=5*/bf16[256...) while((s32[]{:T(128)}, ...), condition=%wide.region_9.10_spmd.clone, body=%wide.region_8.9_spmd.clone.sunk | while | flops 426459680 | bytes 15725944 | solution.py:212
  309.2 20.5 collective-permute-done.1
  337.3 20.5 collective-permute-done.1
  365.4 20.5 collective-permute-done.1
  401.2 305.5 %all-gather.9.cloned.1.call-done = bf16[1600,6400]{1,0:T(8,128)(2,1)} async-done(((bf16[200,6400]{1,0:T(8,128)(2,1)}), bf16[1600,6400]{1,0:T(8,128)(2,1)}) %all-gather.9.cloned.1.call-update) | async-done | bytes 20480016 | tf_op jit(solution)/shard_map/all_gather | solution.py:219
  706.8 12.5 convolution_add_fusion
  719.2 396.8 %all-gather.11.cloned.1.call-done = bf16[6400,1600]{1,0:T(8,128)(2,1)} async-done(((bf16[800,1600]{1,0:T(8,128)(2,1)}), bf16[6400,1600]{1,0:T(8,128)(2,1)}) %all-gather.11.cloned.1.call-update) | async-done | bytes 20480016 | tf_op jit(solution)/shard_map/all_gather | solution.py:241
  1116.1 15.6 fusion.88
  1131.7 13.8 multiply_reduce_fusion
  1165.0 125.4 %while.60 = (s32[]{:T(128)}, bf16[256,2,25,64]{0,3,2,1:T(8,128)(2,1)}, bf16[256,2,25,64]{0,3,2,1:T(8,128)(2,1)}, f32[256,25,64]{0,2,1:T(8,128)}, s32[]{:T(128)},...) while((s32[]{:T(128)}, ...), condition=%wide.region_15.16_spmd.clone, body=%wide.region_14.15_spmd.clone.sunk | while | flops 1070350848 | bytes 81393160 | solution.py:312
  1167.4 18.8 collective-permute-done.2
  1209.0 18.8 collective-permute-done.2
  1250.6 18.8 collective-permute-done.2
  1292.1 19.0 collective-permute-done.11
  1320.9 12.8 convolution_convert_fusion.1
  1334.9 13.6 convolution_convert_fusion
  1353.3 129.1 %collective-permute-done.4 = bf16[800,1600]{1,0:T(8,128)(2,1)S(1)} collective-permute-done((bf16[800,1600]{1,0:T(8,128)(2,1)}, bf16[800,1600]{1,0:T(8,128)(2,1)S(1)}, u32[]{:S(2)}, u32[]{:S(2)}) %collective-permute-start.4) | collective-permute-done | bytes 2560032 | tf_op jit(solution)/shard_map/ppermute | solution.py:20
  1490.6 165.4 %collective-permute-done.6 = bf16[800,1600]{1,0:T(8,128)(2,1)S(1)} collective-permute-done((bf16[800,1600]{1,0:T(8,128)(2,1)S(1)}, bf16[800,1600]{1,0:T(8,128)(2,1)S(1)}, u32[]{:S(2)}, u32[]{:S(2)}) %collective-permute-start.6) | collective-permute-done | bytes 2560032 | tf_op jit(solution)/shard_map/ppermute | solution.py:20
  1667.7 107.4 %collective-permute-done.8 = bf16[800,1600]{1,0:T(8,128)(2,1)} collective-permute-done((bf16[800,1600]{1,0:T(8,128)(2,1)S(1)}, bf16[800,1600]{1,0:T(8,128)(2,1)}, u32[]{:S(2)}, u32[]{:S(2)}) %collective-permute-start.8) | collective-permute-done | bytes 2560032 | tf_op jit(solution)/shard_map/ppermute | solution.py:20
  1807.6 56.9 %collective-permute-done.10 = bf16[800,1600]{1,0:T(8,128)(2,1)} collective-permute-done((bf16[800,1600]{1,0:T(8,128)(2,1)}, bf16[800,1600]{1,0:T(8,128)(2,1)}, u32[]{:S(2)}, u32[]{:S(2)}) %collective-permute-start.10) | collective-permute-done | bytes 2560032 | tf_op jit(solution)/shard_map/ppermute | solution.py:20
  1879.9 380.1 %reduce-scatter.15.cloned.1.call-done = bf16[200,6400]{1,0:T(8,128)(2,1)} async-done(((bf16[1600,6400]{1,0:T(8,128)(2,1)}), bf16[200,6400]{1,0:T(8,128)(2,1)}) %reduce-scatter.15.cloned.1.call-update) | async-done | bytes 2560016
  2260.0 351.1 %reduce-scatter.11.cloned.1.call-done = bf16[800,1600]{1,0:T(8,128)(2,1)} async-done(((bf16[6400,1600]{1,0:T(8,128)(2,1)}), bf16[800,1600]{1,0:T(8,128)(2,1)}) %reduce-scatter.11.cloned.1.call-update) | async-done | bytes 2560016 | tf_op jit(solution)/shard_map/reduce_scatter | solution.py:259
  2612.7 35.7 %all-reduce.21 = (bf16[1600]{0:T(1024)(128)(2,1)S(1)}, bf16[1600]{0:T(1024)(128)(2,1)S(1)}, bf16[1600]{0:T(1024)(128)(2,1)S(1)}, bf16[1600]{0:T(1024)(128)(2,1)S...) all-reduce(bf16[1600]{0:T(1024)(128)(2,1)S(1)} %dynamic-update-slic, ...), channel_id=1, replica_groups=mesh['ctx'=4,'fsdp'=8] {'fsdp'}, use_global_device_ids=true, to_apply=%add.9 | all-reduce | flops 20800 | bytes 83200
  2665.0 17.4 fusion.44
  2682.4 76.2 %all-reduce.27.cloned.1.call-done = (bf16[200,4800]{1,0:T(8,128)(2,1)}, bf16[200,1600]{1,0:T(8,128)(2,1)}, bf16[200,6400]{1,0:T(8,128)(2,1)}, bf16[800,1600]{1,0:T(8,128)(2,1)}) async-done(((bf16[200,4800]{1,0:T(8,128)(2,1)}, bf16[200,1600]{1,0:T(8,128)(2,1)}, bf16[200,6400]{1,0:T(8,128)(2,1)}, bf16[800,1600]{1,0:T(8,128)(2,1)}), (bf16[200,4800]{1,0:T(8,128)(2,1)}, bf16[200,1600]{1,0:T(8,128)(2,1)}, ...) | async-done | bytes 7680016 | tf_op jit(solution)/shard_map/psum | solution.py:362
  (358 shorter events, 269.0 us)
Async XLA Ops:
  7.2 219.6 %all-gather.5.cloned.1.call-start = ((), (), s32[]{:S(2)}) async-start(), calls=%async_computation.4 | async-start | bytes 17510400 | tf_op jit(solution)/shard_map/all_gather | solution.py:147
  8.0 387.8 %all-gather.7.cloned.1.call-start = ((), (), s32[]{:S(2)}) async-start(), calls=%async_computation.5 | async-start | bytes 5990400 | tf_op jit(solution)/shard_map/all_gather | solution.py:148
  8.8 698.0 %all-gather.9.cloned.1.call-start = ((), (), s32[]{:S(2)}) async-start(), calls=%async_computation.6 | async-start | bytes 23040000 | tf_op jit(solution)/shard_map/all_gather | solution.py:219
  9.5 1106.6 %all-gather.11.cloned.1.call-start = ((), (), s32[]{:S(2)}) async-start(), calls=%async_computation.7 | async-start | bytes 23961600 | tf_op jit(solution)/shard_map/all_gather | solution.py:241
  10.1 1869.8 %reduce-scatter.13.cloned.1.call-start = ((), (), s32[]{:S(2)}) async-start(), calls=%async_computation.10 | async-start | bytes 5990400
  55.0 186.5 %copy-start.30 = (f32[1600]{0:T(1024)}, f32[1600]{0:T(1024)S(1)}, u32[]{:S(2)}) copy-start(f32[1600]{0:T(1024)S(1)} %convert_element_type.233) | copy-start | bytes 19204
  256.3 12.0 collective-permute-start
  272.0 12.0 collective-permute-start
  287.7 12.0 collective-permute-start
  309.0 20.8 collective-permute-start.1
  337.0 20.8 collective-permute-start.1
  365.1 20.8 collective-permute-start.1
  401.0 744.6 %copy-start.2 = (f32[256,1600]{0,1:T(8,128)}, f32[256,1600]{0,1:T(8,128)S(1)}, u32[]{:S(2)}) copy-start(f32[256,1600]{0,1:T(8,128)S(1)} %get-tuple-element.873) | copy-start | bytes 4915204
  1163.6 716.3 %reduce-scatter.9.cloned.1.call-start = ((), (), s32[]{:S(2)}) async-start(), calls=%async_computation.8 | async-start | bytes 17510400 | tf_op jit(solution)/shard_map/reduce_scatter | solution.py:339
  1165.4 20.8 collective-permute-start.2
  1165.5 38.4 %collective-permute-start.3 = (bf16[256,2,25,64]{0,3,2,1:T(8,128)(2,1)}, bf16[256,2,25,64]{0,3,2,1:T(8,128)(2,1)}, u32[]{:S(2)}, u32[]{:S(2)}) collective-permute-start(bf16[256,2,25,64]{0,3,2,1:T(8,128)(2,1)} %get-tuple-element.1158), channel_id=1, source_target_pairs={{24,0},{0,8},{8,16},{16,24},{25,1},{1,9},{9,17},{17,25},{26,2},{2,... | collective-permute-start | bytes 4915208 | tf_op jit(solution)/shard_map/while/body/eval_jaxpr/ppermute | solution.py:33
  1207.1 20.8 collective-permute-start.2
  1207.1 38.4 %collective-permute-start.3 = (bf16[256,2,25,64]{0,3,2,1:T(8,128)(2,1)}, bf16[256,2,25,64]{0,3,2,1:T(8,128)(2,1)}, u32[]{:S(2)}, u32[]{:S(2)}) collective-permute-start(bf16[256,2,25,64]{0,3,2,1:T(8,128)(2,1)} %get-tuple-element.1158), channel_id=1, source_target_pairs={{24,0},{0,8},{8,16},{16,24},{25,1},{1,9},{9,17},{17,25},{26,2},{2,... | collective-permute-start | bytes 4915208 | tf_op jit(solution)/shard_map/while/body/eval_jaxpr/ppermute | solution.py:33
  1248.7 20.8 collective-permute-start.2
  1248.7 38.4 %collective-permute-start.3 = (bf16[256,2,25,64]{0,3,2,1:T(8,128)(2,1)}, bf16[256,2,25,64]{0,3,2,1:T(8,128)(2,1)}, u32[]{:S(2)}, u32[]{:S(2)}) collective-permute-start(bf16[256,2,25,64]{0,3,2,1:T(8,128)(2,1)} %get-tuple-element.1158), channel_id=1, source_target_pairs={{24,0},{0,8},{8,16},{16,24},{25,1},{1,9},{9,17},{17,25},{26,2},{2,... | collective-permute-start | bytes 4915208 | tf_op jit(solution)/shard_map/while/body/eval_jaxpr/ppermute | solution.py:33
  1290.4 20.8 collective-permute-start.11
  1319.5 940.5 %reduce-scatter.15.cloned.1.call-start = ((), (), s32[]{:S(2)}) async-start(), calls=%async_computation.11 | async-start | bytes 23040000
  1333.7 1277.4 %reduce-scatter.11.cloned.1.call-start = ((), (), s32[]{:S(2)}) async-start(), calls=%async_computation.9 | async-start | bytes 23961600 | tf_op jit(solution)/shard_map/reduce_scatter | solution.py:259
  1348.5 430.9 %copy-start.56 = (bf16[200]{0:T(256)(128)(2,1)S(1)}, bf16[200]{0:T(256)(128)(2,1)}, u32[]{:S(2)}) copy-start(bf16[200]{0:T(256)(128)(2,1)} %param.33) | copy-start | bytes 1204
  1348.5 1410.1 %all-reduce.27.cloned.1.call-start = ((), (), s32[]{:S(2)}) async-start(), calls=%async_computation.12 | async-start | bytes 15667200 | tf_op jit(solution)/shard_map/psum | solution.py:362
  1348.6 133.9 %collective-permute-start.4 = (bf16[800,1600]{1,0:T(8,128)(2,1)}, bf16[800,1600]{1,0:T(8,128)(2,1)S(1)}, u32[]{:S(2)}, u32[]{:S(2)}) collective-permute-start(bf16[800,1600]{1,0:T(8,128)(2,1)} %param.31), channel_id=1, source_target_pairs={{0,1},{1,2},{2,3},{3,4},{4,5},{5,6},{6,7},{7,0},{8,9},{9,10},{10,1... | collective-permute-start | bytes 7680008 | tf_op jit(solution)/shard_map/ppermute | solution.py:20
  1349.3 137.4 %collective-permute-start.5 = (bf16[800,1600]{1,0:T(8,128)(2,1)}, bf16[800,1600]{1,0:T(8,128)(2,1)S(1)}, u32[]{:S(2)}, u32[]{:S(2)}) collective-permute-start(bf16[800,1600]{1,0:T(8,128)(2,1)} %param.31), channel_id=1, source_target_pairs={{0,7},{1,0},{2,1},{3,2},{4,3},{5,4},{6,5},{7,6},{8,15},{9,8},{10,9... | collective-permute-start | bytes 7680008 | tf_op jit(solution)/shard_map/ppermute | solution.py:23
  1483.9 172.1 %collective-permute-start.6 = (bf16[800,1600]{1,0:T(8,128)(2,1)S(1)}, bf16[800,1600]{1,0:T(8,128)(2,1)S(1)}, u32[]{:S(2)}, u32[]{:S(2)}) collective-permute-start(bf16[800,1600]{1,0:T(8,128)(2,1)S(1)} %collective-permute-done.4), channel_id=1, source_target_pairs={{0,1},{1,2},{2,3},{3,4},{4,5},{5,6},{6,7},{7,0},{8,9},{9,10},{10,1... | collective-permute-start | bytes 7680008 | tf_op jit(solution)/shard_map/ppermute | solution.py:20
  1486.6 175.4 %collective-permute-start.7 = (bf16[800,1600]{1,0:T(8,128)(2,1)S(1)}, bf16[800,1600]{1,0:T(8,128)(2,1)}, u32[]{:S(2)}, u32[]{:S(2)}) collective-permute-start(bf16[800,1600]{1,0:T(8,128)(2,1)S(1)} %collective-permute-done.5), channel_id=1, source_target_pairs={{0,7},{1,0},{2,1},{3,2},{4,3},{5,4},{6,5},{7,6},{8,15},{9,8},{10,9... | collective-permute-start | bytes 7680008 | tf_op jit(solution)/shard_map/ppermute | solution.py:23
  1656.0 119.1 %collective-permute-start.8 = (bf16[800,1600]{1,0:T(8,128)(2,1)S(1)}, bf16[800,1600]{1,0:T(8,128)(2,1)}, u32[]{:S(2)}, u32[]{:S(2)}) collective-permute-start(bf16[800,1600]{1,0:T(8,128)(2,1)S(1)} %collective-permute-done.6), channel_id=1, source_target_pairs={{0,1},{1,2},{2,3},{3,4},{4,5},{5,6},{6,7},{7,0},{8,9},{9,10},{10,1... | collective-permute-start | bytes 7680008 | tf_op jit(solution)/shard_map/ppermute | solution.py:20
  1662.0 142.1 %collective-permute-start.9 = (bf16[800,1600]{1,0:T(8,128)(2,1)}, bf16[800,1600]{1,0:T(8,128)(2,1)}, u32[]{:S(2)}, u32[]{:S(2)}) collective-permute-start(bf16[800,1600]{1,0:T(8,128)(2,1)} %collective-permute-done.7), channel_id=1, source_target_pairs={{0,7},{1,0},{2,1},{3,2},{4,3},{5,4},{6,5},{7,6},{8,15},{9,8},{10,9... | collective-permute-start | bytes 7680008 | tf_op jit(solution)/shard_map/ppermute | solution.py:23
  1775.2 89.3 %collective-permute-start.10 = (bf16[800,1600]{1,0:T(8,128)(2,1)}, bf16[800,1600]{1,0:T(8,128)(2,1)}, u32[]{:S(2)}, u32[]{:S(2)}) collective-permute-start(bf16[800,1600]{1,0:T(8,128)(2,1)} %collective-permute-done.8), channel_id=1, source_target_pairs={{0,1},{1,2},{2,3},{3,4},{4,5},{5,6},{6,7},{7,0},{8,9},{9,10},{10,1... | collective-permute-start | bytes 7680008 | tf_op jit(solution)/shard_map/ppermute | solution.py:20
  (62 other events, 2035.8 us)
Sparse Core Ops, SparseCore 0:
  10.2 216.5 all-gather.4
  228.9 85.4 all-gather.6
  316.0 390.7 all-gather.8
  708.1 407.8 all-gather.10
  1163.7 123.8 reduce-scatter.12
  1319.6 489.2 reduce-scatter.8
  1812.4 447.5 reduce-scatter.14
  2263.7 347.4 reduce-scatter.10
  2613.8 144.8 all-reduce.26
